TPU v7x, 32 devices: a whole 2x2x4 slice. The times are simulated.
32 devices in a mesh: tm: 4 (over y, x), space: 8 (over z, core).
Axes of the slice: x: 2, y: 2, z: 4, core: 2. Of those that a mesh axis runs over, the one named last changes fastest.
Arguments:
- forcing: float32 [4, 64, 16384], P('tm', 'space'), may hold values from -6 to 6
- conductivity: float32 [64, 16384], P('space'), may hold values from 0.1 to 1
Outputs:
- solution: float32 [4, 64, 16384], P('tm', 'space')
All inputs are finite; a program needn't handle non-finite values.
Results may differ from a plain program's by a relative error of at most 0.0001.
Values sent between devices are 32-bit elements; how exact they have to be, the bound alone decides.
A program may use at most 64 MiB of HBM per device.

v0:
```python
import functools

import jax
import jax.numpy as jnp
from jax import lax
from jax.experimental import pallas as pl
from jax.experimental.pallas import tpu as pltpu
from jax.sharding import PartitionSpec as P

MESH = pl.DeviceIdType.MESH
LANES = 128
SUB = 8


def kernel(
    ntm, nsp, f_hbm, k_hbm, out_hbm,
    fwin, kwin, scl, inv, gn, gs, gw, ge, tau, abuf, bbuf, q0, q1, q2, res, part, red,
    f_send, f_recv, k_send, k_recv, r_send, r_recv, o_send, o_recv, own_sem,
):
    n = ntm * nsp
    mt, ms = lax.axis_index("tm"), lax.axis_index("space")
    me = mt * nsp + ms
    tl, tiles, rows, _ = f_hbm.shape
    steps, width = fwin.shape[0], fwin.shape[1]
    nx = scl.shape[1] - 2 * SUB
    blocks = nx // SUB
    own = tiles // n

    def start_of(d):
        return jnp.minimum(jnp.maximum(d * own - 1, 0), tiles - width)

    def strip(s):
        return pl.ds(pl.multiple_of(SUB + s * rows, SUB), rows)

    def f_copy(d):
        return pltpu.make_async_remote_copy(
            src_ref=f_hbm.at[:, pl.ds(start_of(d), width)],
            dst_ref=fwin.at[pl.ds(mt * tl, tl), :, strip(ms)],
            send_sem=f_send.at[d], recv_sem=f_recv.at[me],
            device_id=(d // nsp, d % nsp), device_id_type=MESH)

    def f_arrival(d):
        return pltpu.make_async_remote_copy(
            src_ref=f_hbm.at[:, pl.ds(0, width)],
            dst_ref=fwin.at[pl.ds((d // nsp) * tl, tl), :, strip(d % nsp)],
            send_sem=f_send.at[d], recv_sem=f_recv.at[d],
            device_id=(d // nsp, d % nsp), device_id_type=MESH)

    def k_copy(s):
        return pltpu.make_async_remote_copy(
            src_ref=k_hbm.at[pl.ds(start_of(mt * nsp + s), width)],
            dst_ref=kwin.at[:, strip(ms)],
            send_sem=k_send.at[s], recv_sem=k_recv.at[ms],
            device_id=(mt, s), device_id_type=MESH)

    def k_arrival(s):
        return pltpu.make_async_remote_copy(
            src_ref=k_hbm.at[pl.ds(0, width)],
            dst_ref=kwin.at[:, strip(s)],
            send_sem=k_send.at[s], recv_sem=k_recv.at[s],
            device_id=(mt, s), device_id_type=MESH)

    def r_copy(d):
        return pltpu.make_async_remote_copy(
            src_ref=part, dst_ref=red.at[me],
            send_sem=r_send.at[d], recv_sem=r_recv.at[me],
            device_id=(d // nsp, d % nsp), device_id_type=MESH)

    def r_arrival(d):
        return pltpu.make_async_remote_copy(
            src_ref=part, dst_ref=red.at[d],
            send_sem=r_send.at[d], recv_sem=r_recv.at[d],
            device_id=(d // nsp, d % nsp), device_id_type=MESH)

    def res_piece(d):
        return res.at[pl.ds((d // nsp) * tl, tl), :,
                      pl.ds(pl.multiple_of((d % nsp) * rows, SUB), rows)]

    def o_copy(d):
        return pltpu.make_async_remote_copy(
            src_ref=res_piece(d), dst_ref=out_hbm.at[:, pl.ds(me * own, own)],
            send_sem=o_send.at[d], recv_sem=o_recv.at[me],
            device_id=(d // nsp, d % nsp), device_id_type=MESH)

    def o_arrival(d):
        return pltpu.make_async_remote_copy(
            src_ref=res_piece(d), dst_ref=out_hbm.at[:, pl.ds(d * own, own)],
            send_sem=o_send.at[d], recv_sem=o_recv.at[d],
            device_id=(d // nsp, d % nsp), device_id_type=MESH)

    def loop(low, high, act):
        def step(j, carry):
            act(j)
            return carry
        lax.fori_loop(low, high, step, 0)

    def peers(act):
        loop(1, n, lambda j: act((me + j) % n))

    def side_peers(act):
        loop(1, nsp, lambda j: act((ms + j) % nsp))

    barrier = pltpu.get_barrier_semaphore()
    peers(lambda d: pl.semaphore_signal(
        barrier, inc=1, device_id=(d // nsp, d % nsp), device_id_type=MESH))
    own_k = pltpu.make_async_copy(
        k_hbm.at[pl.ds(start_of(me), width)], kwin.at[:, strip(ms)], own_sem.at[0])
    own_f = pltpu.make_async_copy(
        f_hbm.at[:, pl.ds(start_of(me), width)],
        fwin.at[pl.ds(mt * tl, tl), :, strip(ms)], own_sem.at[1])
    own_k.start()
    own_f.start()
    zero = jnp.zeros((SUB, LANES), jnp.float32)
    for edge in (0, SUB + nx):
        for c in range(width):
            for ref in (kwin, scl):
                ref[c, edge:edge + SUB, :] = zero
            for ref in (tau, abuf, bbuf, q0, q1, q2):
                for s in range(steps):
                    ref[s, c, edge:edge + SUB, :] = zero
    pl.semaphore_wait(barrier, n - 1)

    side_peers(lambda s: k_copy(s).start())
    peers(lambda d: f_copy(d).start())
    own_k.wait()
    side_peers(lambda s: k_arrival(s).wait_recv())

    lane = lax.broadcasted_iota(jnp.int32, (SUB, LANES), 1)
    first, last = lane == 0, lane == LANES - 1

    def lefts(xs):
        turned = [pltpu.roll(x, 1, 1) for x in xs]
        return [jnp.where(first, turned[c - 1] if c else 0.0, turned[c]) for c in range(width)]

    def rights(xs):
        turned = [pltpu.roll(x, LANES - 1, 1) for x in xs] + [0.0]
        return [jnp.where(last, turned[c + 1], turned[c]) for c in range(width)]

    def near(i, offset):
        return pl.ds(SUB + SUB * i + offset, SUB)

    def at(i):
        return pl.ds(pl.multiple_of(SUB + SUB * i, SUB), SUB)

    def flat(i):
        return pl.ds(pl.multiple_of(SUB * i, SUB), SUB)

    def weights_first(i):
        ks = [kwin[c, at(i), :] for c in range(width)]
        for c, (k, l, r) in enumerate(zip(ks, lefts(ks), rights(ks))):
            up, down = kwin[c, near(i, -1), :], kwin[c, near(i, 1), :]
            diag = 1.0 + 0.5 * (k + up) + 0.5 * (k + down) + 0.5 * (k + l) + 0.5 * (k + r)
            scl[c, at(i), :] = 1.0 / jnp.sqrt(diag)
            inv[c, flat(i), :] = 1.0 / diag

    def weights_second(i):
        ks = [kwin[c, at(i), :] for c in range(width)]
        ss = [scl[c, at(i), :] for c in range(width)]
        quads = zip(ks, lefts(ks), rights(ks), ss, lefts(ss), rights(ss))
        for c, (k, kl, kr, s, sl, sr) in enumerate(quads):
            half = 0.5 * s
            gn[c, flat(i), :] = half * (k + kwin[c, near(i, -1), :]) * scl[c, near(i, -1), :]
            gs[c, flat(i), :] = half * (k + kwin[c, near(i, 1), :]) * scl[c, near(i, 1), :]
            gw[c, flat(i), :] = half * (k + kl) * sl
            ge[c, flat(i), :] = half * (k + kr) * sr

    loop(0, blocks, weights_first)
    loop(0, blocks, weights_second)

    own_f.wait()
    peers(lambda d: f_arrival(d).wait_recv())

    def scale_in(i):
        for c in range(width):
            s = scl[c, at(i), :]
            for t in range(steps):
                tau[t, c, at(i), :] = s * fwin[steps - 1 - t, c, at(i), :]

    loop(0, blocks, scale_in)

    offset = me * own - start_of(me)
    mine = [jnp.where(jnp.logical_and(c >= offset, c < offset + own), 1.0, 0.0)
            for c in range(width)]

    def sweep(src, use):
        def block(i, total):
            xs = [[src[t, c, at(i), :] for c in range(width)] for t in range(steps)]
            ls = [lefts(x) for x in xs]
            rs = [rights(x) for x in xs]
            for c in range(width):
                wn, wso = gn[c, flat(i), :], gs[c, flat(i), :]
                ww, we = gw[c, flat(i), :], ge[c, flat(i), :]
                out = [
                    wn * src[t, c, near(i, -1), :] + wso * src[t, c, near(i, 1), :]
                    + (ww * ls[t][c] + we * rs[t][c])
                    for t in range(steps)
                ]
                term = use(c, i, [xs[t][c] for t in range(steps)], out)
                if term is not None:
                    total = total + mine[c] * term
            return total
        return lax.fori_loop(0, blocks, block, zero)

    def precondition(q):
        def one(c, i, x, g):
            for t in range(steps):
                abuf[t, c, at(i), :] = 0.5 * (x[t] + g[t])

        def two(c, i, x, g):
            for t in range(steps):
                bbuf[t, c, at(i), :] = 0.125 * tau[t, c, at(i), :] + g[t]

        def three(c, i, x, g):
            term = zero
            for t in range(steps):
                v = tau[t, c, at(i), :]
                y = 0.75 * v + g[t]
                q[t, c, at(i), :] = y
                term = term + v * y
            return term

        sweep(tau, one)
        sweep(abuf, two)
        return sweep(bbuf, three)

    def operate(q):
        def use(c, i, x, g):
            shrink = inv[c, flat(i), :]
            term = zero
            for t in range(steps):
                y = x[t] - g[t]
                if t:
                    y = y - shrink * x[t - 1]
                tau[steps - 1 - t, c, at(i), :] = y
                term = term + y * x[steps - 1 - t]
            return term
        return sweep(q, use)

    precondition(q0)
    m1 = operate(q0)
    m2 = precondition(q1)
    m3 = operate(q1)
    m4 = precondition(q2)
    m5 = operate(q2)

    def norm_one(c, i, x, g):
        term = zero
        for t in range(steps):
            abuf[t, c, at(i), :] = g[t]
            term = term + (x[t] * (0.75 * x[t] + 0.125 * g[t]) + 0.5 * (g[t] * g[t]))
        return term

    def norm_two(c, i, x, g):
        term = zero
        for t in range(steps):
            term = term + 0.5 * (x[t] * g[t])
        return term

    m6 = sweep(tau, norm_one) + sweep(abuf, norm_two)

    row = jnp.zeros((1, LANES), jnp.float32)
    lane1 = lax.broadcasted_iota(jnp.int32, (1, LANES), 1)
    for j, m in enumerate((m1, m2, m3, m4, m5, m6)):
        value = jnp.sum(jnp.sum(m, axis=0, keepdims=True), axis=1, keepdims=True)
        row = jnp.where(lane1 == j, value, row)
    part[...] = row
    red[me] = row
    peers(lambda d: r_copy(d).start())
    peers(lambda d: r_arrival(d).wait_recv())
    total = lax.fori_loop(0, n, lambda j, acc: acc + red[j], jnp.zeros((1, LANES), jnp.float32))
    n1, n2, n3, n4, n5, n6 = [
        jnp.sum(jnp.where(lane1 == j, total, 0.0), axis=1, keepdims=True) for j in range(6)]

    tiny = 1e-7
    d1 = jnp.maximum(n2, 1e-37)
    l21, l31 = n3 / d1, n4 / d1
    d2 = jnp.maximum(n4 - l21 * n3, jnp.maximum(tiny * n4, 1e-37))
    e32 = n5 - l31 * n3
    l32 = e32 / d2
    d3 = jnp.maximum(n6 - l31 * n4 - l32 * e32, jnp.maximum(tiny * n6, 1e-37))
    y2 = n2 - l21 * n1
    y3 = n3 - l31 * n1 - l32 * y2
    a2 = y3 / d3
    a1 = y2 / d2 - l32 * a2
    a0 = n1 / d1 - l21 * a1 - l31 * a2

    def finish(i):
        for c in range(own):
            s = scl[offset + c, at(i), :]
            s0, s1, s2 = a0 * s, a1 * s, a2 * s
            for t in range(steps):
                res[t, c, flat(i), :] = (
                    s0 * q0[t, offset + c, at(i), :] + s1 * q1[t, offset + c, at(i), :]
                    + s2 * q2[t, offset + c, at(i), :])

    loop(0, blocks, finish)
    own_out = pltpu.make_async_copy(
        res_piece(me), out_hbm.at[:, pl.ds(me * own, own)], own_sem.at[2])
    own_out.start()
    peers(lambda d: o_copy(d).start())
    side_peers(lambda s: k_copy(s).wait_send())
    peers(lambda d: f_copy(d).wait_send())
    peers(lambda d: r_copy(d).wait_send())
    own_out.wait()
    peers(lambda d: o_arrival(d).wait_recv())
    peers(lambda d: o_copy(d).wait_send())


def solution(mesh):
    ntm, nsp = mesh.shape["tm"], mesh.shape["space"]
    n = ntm * nsp

    def body(forcing, conductivity):
        tl, rows, columns = forcing.shape
        tiles = columns // LANES
        own = tiles // n
        width = min(own + 2, tiles)
        steps, nx = tl * ntm, rows * nsp
        f = forcing.reshape(tl, rows, tiles, LANES).transpose(0, 2, 1, 3)
        k = conductivity.reshape(rows, tiles, LANES).transpose(1, 0, 2)
        padded = pltpu.VMEM((width, nx + 2 * SUB, LANES), jnp.float32)
        plain = pltpu.VMEM((width, nx, LANES), jnp.float32)
        field = pltpu.VMEM((steps, width, nx + 2 * SUB, LANES), jnp.float32)
        dma = pltpu.SemaphoreType.DMA
        out = pl.pallas_call(
            functools.partial(kernel, ntm, nsp),
            out_shape=jax.ShapeDtypeStruct((tl, tiles, rows, LANES), jnp.float32),
            in_specs=[pl.BlockSpec(memory_space=pltpu.HBM)] * 2,
            out_specs=pl.BlockSpec(memory_space=pltpu.HBM),
            scratch_shapes=[
                field, padded, padded, plain, plain, plain, plain, plain,
                field, field, field, field, field, field,
                pltpu.VMEM((steps, own, nx, LANES), jnp.float32),
                pltpu.VMEM((1, LANES), jnp.float32),
                pltpu.VMEM((n, 1, LANES), jnp.float32),
                dma((n,)), dma((n,)), dma((nsp,)), dma((nsp,)),
                dma((n,)), dma((n,)), dma((n,)), dma((n,)), dma((3,)),
            ],
            compiler_params=pltpu.CompilerParams(collective_id=0, has_side_effects=True),
        )(f, k)
        return out.transpose(0, 2, 1, 3).reshape(tl, rows, columns)

    return jax.shard_map(
        body,
        mesh=mesh,
        in_specs=(P("tm", "space", None), P("space", None)),
        out_specs=P("tm", "space", None),
        check_vma=False,
    )
```

profile of v0, /device:TPU:0, one launch (start us, length us, event | category | flops | bytes accessed | tf_op | source)
XLA Modules:
  0.0 66.4 jit_solution(8065178812911832137)
XLA Ops:
  0.0 64.5 %shard_map.28 = f32[1,128,8,128]{3,2,1,0:T(8,128)} custom-call(f32[1,128,8,128]{3,2,1,0:T(8,128)} %bitcast.10, f32[128,8,128]{2,1,0:T(8,128)} %bitcast.11), custom_call_target="tpu_custom_call" | custom-call | tf_op jit(solution)/shard_map/pallas_call | solution.py:325
  64.6 1.9 %copy.4 = f32[1,8,16384]{2,1,0:T(8,128)} copy(f32[1,8,16384]{2,1,0:T(8,128)} %bitcast.9) | data formatting | bytes 1048576
where the time goes:
time: 66.6 us; the launch traced here: 66.4 us
  Pallas kernels  64.5 us (97%)
  local copies, waits for them, and re-layouts  1.87 us (3%)
    pallas_call x1, Pallas kernels, body(): pl.pallas_call(functools.partial(kernel, ntm, nsp), out_shape=jax.ShapeDt...  64.5 us
    unnamed x1, local copies, waits for them, and re-layouts  1.87 us

commit v1 on v0

--- a/solution.py
+++ b/solution.py
@@ -14,48 +14,44 @@
 
 def kernel(
     ntm, nsp, f_hbm, k_hbm, out_hbm,
-    fwin, kwin, scl, inv, gn, gs, gw, ge, tau, abuf, bbuf, q0, q1, q2, res, part, red,
+    fstage, kloc, kstage, fwin, kwin, scl, inv, gn, gs, gw, ge, tau, abuf, bbuf, q0, q1, q2, res, part, red,
     f_send, f_recv, k_send, k_recv, r_send, r_recv, o_send, o_recv, own_sem,
 ):
     n = ntm * nsp
     mt, ms = lax.axis_index("tm"), lax.axis_index("space")
     me = mt * nsp + ms
-    tl, tiles, rows, _ = f_hbm.shape
+    tl, _, own, rows, _ = f_hbm.shape
     steps, width = fwin.shape[0], fwin.shape[1]
     nx = scl.shape[1] - 2 * SUB
     blocks = nx // SUB
-    own = tiles // n
-
-    def start_of(d):
-        return jnp.minimum(jnp.maximum(d * own - 1, 0), tiles - width)
 
     def strip(s):
         return pl.ds(pl.multiple_of(SUB + s * rows, SUB), rows)
 
     def f_copy(d):
         return pltpu.make_async_remote_copy(
-            src_ref=f_hbm.at[:, pl.ds(start_of(d), width)],
+            src_ref=fstage.at[:, d],
             dst_ref=fwin.at[pl.ds(mt * tl, tl), :, strip(ms)],
             send_sem=f_send.at[d], recv_sem=f_recv.at[me],
             device_id=(d // nsp, d % nsp), device_id_type=MESH)
 
     def f_arrival(d):
         return pltpu.make_async_remote_copy(
-            src_ref=f_hbm.at[:, pl.ds(0, width)],
+            src_ref=fstage.at[:, d],
             dst_ref=fwin.at[pl.ds((d // nsp) * tl, tl), :, strip(d % nsp)],
             send_sem=f_send.at[d], recv_sem=f_recv.at[d],
             device_id=(d // nsp, d % nsp), device_id_type=MESH)
 
     def k_copy(s):
         return pltpu.make_async_remote_copy(
-            src_ref=k_hbm.at[pl.ds(start_of(mt * nsp + s), width)],
+            src_ref=kstage.at[s],
             dst_ref=kwin.at[:, strip(ms)],
             send_sem=k_send.at[s], recv_sem=k_recv.at[ms],
             device_id=(mt, s), device_id_type=MESH)
 
     def k_arrival(s):
         return pltpu.make_async_remote_copy(
-            src_ref=k_hbm.at[pl.ds(0, width)],
+            src_ref=kstage.at[s],
             dst_ref=kwin.at[:, strip(s)],
             send_sem=k_send.at[s], recv_sem=k_recv.at[s],
             device_id=(mt, s), device_id_type=MESH)
@@ -103,13 +99,14 @@
     barrier = pltpu.get_barrier_semaphore()
     peers(lambda d: pl.semaphore_signal(
         barrier, inc=1, device_id=(d // nsp, d % nsp), device_id_type=MESH))
-    own_k = pltpu.make_async_copy(
-        k_hbm.at[pl.ds(start_of(me), width)], kwin.at[:, strip(ms)], own_sem.at[0])
-    own_f = pltpu.make_async_copy(
-        f_hbm.at[:, pl.ds(start_of(me), width)],
-        fwin.at[pl.ds(mt * tl, tl), :, strip(ms)], own_sem.at[1])
-    own_k.start()
-    own_f.start()
+    loads = [
+        pltpu.make_async_copy(f_hbm, fstage.at[:, :, pl.ds(0, own)], own_sem.at[0]),
+        pltpu.make_async_copy(k_hbm, kloc, own_sem.at[1]),
+        pltpu.make_async_copy(
+            k_hbm.at[pl.ds(mt * nsp, nsp)], kstage.at[:, pl.ds(0, own)], own_sem.at[2]),
+    ]
+    for load in loads:
+        load.start()
     zero = jnp.zeros((SUB, LANES), jnp.float32)
     for edge in (0, SUB + nx):
         for c in range(width):
@@ -118,23 +115,56 @@
             for ref in (tau, abuf, bbuf, q0, q1, q2):
                 for s in range(steps):
                     ref[s, c, edge:edge + SUB, :] = zero
+    lane = lax.broadcasted_iota(jnp.int32, (SUB, LANES), 1)
+    first, last, ahead = lane == 0, lane == LANES - 1, lane < LANES // 2
+
+    def beside(d, right, left):
+        return jnp.where(ahead, right * jnp.where(d < n - 1, 1.0, 0.0),
+                         left * jnp.where(d > 0, 1.0, 0.0))
+
+    def after(d):
+        return jnp.minimum(d + 1, n - 1)
+
+    def before(d):
+        return jnp.maximum(d - 1, 0)
+
+    for load in loads:
+        load.wait()
+
+    def overlap_k(s):
+        d = mt * nsp + s
+        for r in range(0, rows, SUB):
+            kstage[s, own, r:r + SUB, :] = beside(
+                d, kloc[after(d), 0, r:r + SUB, :], kloc[before(d), own - 1, r:r + SUB, :])
+
+    def overlap_f(d):
+        for t in range(tl):
+            for r in range(0, rows, SUB):
+                fstage[t, d, own, r:r + SUB, :] = beside(
+                    d, fstage[t, after(d), 0, r:r + SUB, :],
+                    fstage[t, before(d), own - 1, r:r + SUB, :])
+
+    loop(0, nsp, overlap_k)
+    loop(0, n, overlap_f)
+    own_k = pltpu.make_async_copy(kstage.at[ms], kwin.at[:, strip(ms)], own_sem.at[0])
+    own_f = pltpu.make_async_copy(
+        fstage.at[:, me], fwin.at[pl.ds(mt * tl, tl), :, strip(ms)], own_sem.at[1])
     pl.semaphore_wait(barrier, n - 1)
 
     side_peers(lambda s: k_copy(s).start())
     peers(lambda d: f_copy(d).start())
+    own_k.start()
+    own_f.start()
     own_k.wait()
     side_peers(lambda s: k_arrival(s).wait_recv())
 
-    lane = lax.broadcasted_iota(jnp.int32, (SUB, LANES), 1)
-    first, last = lane == 0, lane == LANES - 1
-
     def lefts(xs):
         turned = [pltpu.roll(x, 1, 1) for x in xs]
-        return [jnp.where(first, turned[c - 1] if c else 0.0, turned[c]) for c in range(width)]
+        return [jnp.where(first, turned[c - 1], turned[c]) for c in range(width)]
 
     def rights(xs):
-        turned = [pltpu.roll(x, LANES - 1, 1) for x in xs] + [0.0]
-        return [jnp.where(last, turned[c + 1], turned[c]) for c in range(width)]
+        turned = [pltpu.roll(x, LANES - 1, 1) for x in xs]
+        return [jnp.where(last, turned[(c + 1) % width], turned[c]) for c in range(width)]
 
     def near(i, offset):
         return pl.ds(SUB + SUB * i + offset, SUB)
@@ -144,13 +174,16 @@
 
     def flat(i):
         return pl.ds(pl.multiple_of(SUB * i, SUB), SUB)
+
+    inside = beside(me, jnp.ones((SUB, LANES), jnp.float32), jnp.ones((SUB, LANES), jnp.float32))
 
     def weights_first(i):
         ks = [kwin[c, at(i), :] for c in range(width)]
         for c, (k, l, r) in enumerate(zip(ks, lefts(ks), rights(ks))):
             up, down = kwin[c, near(i, -1), :], kwin[c, near(i, 1), :]
             diag = 1.0 + 0.5 * (k + up) + 0.5 * (k + down) + 0.5 * (k + l) + 0.5 * (k + r)
-            scl[c, at(i), :] = 1.0 / jnp.sqrt(diag)
+            scale = 1.0 / jnp.sqrt(diag)
+            scl[c, at(i), :] = scale * inside if c == own else scale
             inv[c, flat(i), :] = 1.0 / diag
 
     def weights_second(i):
@@ -178,26 +211,31 @@
 
     loop(0, blocks, scale_in)
 
-    offset = me * own - start_of(me)
-    mine = [jnp.where(jnp.logical_and(c >= offset, c < offset + own), 1.0, 0.0)
-            for c in range(width)]
-
     def sweep(src, use):
         def block(i, total):
-            xs = [[src[t, c, at(i), :] for c in range(width)] for t in range(steps)]
-            ls = [lefts(x) for x in xs]
-            rs = [rights(x) for x in xs]
+            xs, down, up = {}, {}, {}
+
+            def fetch(c, t):
+                if (c, t) not in xs:
+                    x = src[t, c, at(i), :]
+                    xs[c, t], down[c, t], up[c, t] = (
+                        x, pltpu.roll(x, 1, 1), pltpu.roll(x, LANES - 1, 1))
+
             for c in range(width):
                 wn, wso = gn[c, flat(i), :], gs[c, flat(i), :]
                 ww, we = gw[c, flat(i), :], ge[c, flat(i), :]
-                out = [
-                    wn * src[t, c, near(i, -1), :] + wso * src[t, c, near(i, 1), :]
-                    + (ww * ls[t][c] + we * rs[t][c])
-                    for t in range(steps)
-                ]
-                term = use(c, i, [xs[t][c] for t in range(steps)], out)
-                if term is not None:
-                    total = total + mine[c] * term
+                out = []
+                for t in range(steps):
+                    for b in (c - 1) % width, c, (c + 1) % width:
+                        fetch(b, t)
+                    left = jnp.where(first, down[(c - 1) % width, t], down[c, t])
+                    right = jnp.where(last, up[(c + 1) % width, t], up[c, t])
+                    out.append(
+                        wn * src[t, c, near(i, -1), :] + wso * src[t, c, near(i, 1), :]
+                        + (ww * left + we * right))
+                term = use(c, i, [xs[c, t] for t in range(steps)], out)
+                if term is not None and c < own:
+                    total = total + term
             return total
         return lax.fori_loop(0, blocks, block, zero)
 
@@ -286,12 +324,12 @@
 
     def finish(i):
         for c in range(own):
-            s = scl[offset + c, at(i), :]
+            s = scl[c, at(i), :]
             s0, s1, s2 = a0 * s, a1 * s, a2 * s
             for t in range(steps):
                 res[t, c, flat(i), :] = (
-                    s0 * q0[t, offset + c, at(i), :] + s1 * q1[t, offset + c, at(i), :]
-                    + s2 * q2[t, offset + c, at(i), :])
+                    s0 * q0[t, c, at(i), :] + s1 * q1[t, c, at(i), :]
+                    + s2 * q2[t, c, at(i), :])
 
     loop(0, blocks, finish)
     own_out = pltpu.make_async_copy(
@@ -314,10 +352,10 @@
         tl, rows, columns = forcing.shape
         tiles = columns // LANES
         own = tiles // n
-        width = min(own + 2, tiles)
+        width = own + 1
         steps, nx = tl * ntm, rows * nsp
-        f = forcing.reshape(tl, rows, tiles, LANES).transpose(0, 2, 1, 3)
-        k = conductivity.reshape(rows, tiles, LANES).transpose(1, 0, 2)
+        f = forcing.reshape(tl, rows, n, own, LANES).transpose(0, 2, 3, 1, 4)
+        k = conductivity.reshape(rows, n, own, LANES).transpose(1, 2, 0, 3)
         padded = pltpu.VMEM((width, nx + 2 * SUB, LANES), jnp.float32)
         plain = pltpu.VMEM((width, nx, LANES), jnp.float32)
         field = pltpu.VMEM((steps, width, nx + 2 * SUB, LANES), jnp.float32)
@@ -326,8 +364,11 @@
             functools.partial(kernel, ntm, nsp),
             out_shape=jax.ShapeDtypeStruct((tl, tiles, rows, LANES), jnp.float32),
             in_specs=[pl.BlockSpec(memory_space=pltpu.HBM)] * 2,
-            out_specs=pl.BlockSpec(memory_space=pltpu.HBM),
+            out_specs=pl.BlockSpec(memory_space=pl.ANY),
             scratch_shapes=[
+                pltpu.VMEM((tl, n, width, rows, LANES), jnp.float32),
+                pltpu.VMEM((n, own, rows, LANES), jnp.float32),
+                pltpu.VMEM((nsp, width, rows, LANES), jnp.float32),
                 field, padded, padded, plain, plain, plain, plain, plain,
                 field, field, field, field, field, field,
                 pltpu.VMEM((steps, own, nx, LANES), jnp.float32),
@@ -336,7 +377,8 @@
                 dma((n,)), dma((n,)), dma((nsp,)), dma((nsp,)),
                 dma((n,)), dma((n,)), dma((n,)), dma((n,)), dma((3,)),
             ],
-            compiler_params=pltpu.CompilerParams(collective_id=0, has_side_effects=True),
+            compiler_params=pltpu.CompilerParams(
+                collective_id=0, has_side_effects=True, vmem_limit_bytes=24 * 1024 * 1024),
         )(f, k)
         return out.transpose(0, 2, 1, 3).reshape(tl, rows, columns)
 

time: 66.6 us -> 62.9 us (0.944)
  Pallas kernels: 64.5 us -> 59.8 us
  local copies, waits for them, and re-layouts: 1.87 us -> 2.88 us
    pallas_call x1, Pallas kernels: 64.5 us -> 59.8 us  [body(): pl.pallas_call(functools.partial(kernel, ntm, nsp), out_shape=jax.ShapeDt...]
    unnamed x1 -> x5, local copies, waits for them, and re-layouts: 1.87 us -> 2.88 us
where the time goes in v1:
time: 62.9 us; the launch traced here: 62.7 us
  Pallas kernels  59.8 us (95%)
  local copies, waits for them, and re-layouts  2.88 us (5%)
    pallas_call x1, Pallas kernels, body(): pl.pallas_call(functools.partial(kernel, ntm, nsp), out_shape=jax.ShapeDt...  59.8 us
    unnamed x5, local copies, waits for them, and re-layouts  2.88 us

profile of v1, /device:TPU:0, one launch (start us, length us, event | category | flops | bytes accessed | tf_op | source)
XLA Modules:
  0.0 62.7 jit_solution(925356088416753787)
XLA Ops:
  0.0 0.0 copy-start
  0.0 1.0 %copy-done = f32[1,8,16384]{2,1,0:T(8,128)S(1)} copy-done((f32[1,8,16384]{2,1,0:T(8,128)S(1)}, f32[1,8,16384]{2,1,0:T(8,128)}, u32[]{:S(2)}) %copy-start) | copy-done | bytes 524312
  1.0 0.0 copy-start.1
  1.0 1.0 %copy-done.1 = f32[8,16384]{1,0:T(8,128)S(1)} copy-done((f32[8,16384]{1,0:T(8,128)S(1)}, f32[8,16384]{1,0:T(8,128)}, u32[]{:S(2)}) %copy-start.1) | copy-done | bytes 524312
  2.1 59.8 %shard_map.28 = f32[1,128,8,128]{3,2,1,0:T(8,128)S(1)} custom-call(f32[1,32,4,8,128]{4,3,2,1,0:T(8,128)S(1)} %bitcast.10, f32[32,4,8,128]{3,2,1,0:T(8,128)S(1)} %bitcast.11), custom_call_target="tpu_custom_call" | custom-call | tf_op jit(solution)/shard_map/pallas_call | solution.py:363
  61.9 0.8 %copy.4 = f32[1,8,16384]{2,1,0:T(8,128)} copy(f32[1,8,16384]{2,1,0:T(8,128)S(1)} %bitcast.9) | data formatting | bytes 1048576
Async XLA Ops:
  0.0 1.0 %copy-start = (f32[1,8,16384]{2,1,0:T(8,128)S(1)}, f32[1,8,16384]{2,1,0:T(8,128)}, u32[]{:S(2)}) copy-start(f32[1,8,16384]{2,1,0:T(8,128)} %param.2) | copy-start | bytes 1572868
  1.0 1.0 %copy-start.1 = (f32[8,16384]{1,0:T(8,128)S(1)}, f32[8,16384]{1,0:T(8,128)}, u32[]{:S(2)}) copy-start(f32[8,16384]{1,0:T(8,128)} %param.3) | copy-start | bytes 1572868

commit v2 on v1

--- a/solution.py
+++ b/solution.py
@@ -15,7 +15,7 @@
 def kernel(
     ntm, nsp, f_hbm, k_hbm, out_hbm,
     fstage, kloc, kstage, fwin, kwin, scl, inv, gn, gs, gw, ge, tau, abuf, bbuf, q0, q1, q2, res, part, red,
-    f_send, f_recv, k_send, k_recv, r_send, r_recv, o_send, o_recv, own_sem,
+    f_sem, k_sem, r_sem, o_sem, own_sem,
 ):
     n = ntm * nsp
     mt, ms = lax.axis_index("tm"), lax.axis_index("space")
@@ -28,61 +28,29 @@
     def strip(s):
         return pl.ds(pl.multiple_of(SUB + s * rows, SUB), rows)
 
-    def f_copy(d):
+    def send(src, dst, sems, dt, ds):
         return pltpu.make_async_remote_copy(
-            src_ref=fstage.at[:, d],
-            dst_ref=fwin.at[pl.ds(mt * tl, tl), :, strip(ms)],
-            send_sem=f_send.at[d], recv_sem=f_recv.at[me],
-            device_id=(d // nsp, d % nsp), device_id_type=MESH)
-
-    def f_arrival(d):
-        return pltpu.make_async_remote_copy(
-            src_ref=fstage.at[:, d],
-            dst_ref=fwin.at[pl.ds((d // nsp) * tl, tl), :, strip(d % nsp)],
-            send_sem=f_send.at[d], recv_sem=f_recv.at[d],
-            device_id=(d // nsp, d % nsp), device_id_type=MESH)
-
-    def k_copy(s):
-        return pltpu.make_async_remote_copy(
-            src_ref=kstage.at[s],
-            dst_ref=kwin.at[:, strip(ms)],
-            send_sem=k_send.at[s], recv_sem=k_recv.at[ms],
-            device_id=(mt, s), device_id_type=MESH)
-
-    def k_arrival(s):
-        return pltpu.make_async_remote_copy(
-            src_ref=kstage.at[s],
-            dst_ref=kwin.at[:, strip(s)],
-            send_sem=k_send.at[s], recv_sem=k_recv.at[s],
-            device_id=(mt, s), device_id_type=MESH)
-
-    def r_copy(d):
-        return pltpu.make_async_remote_copy(
-            src_ref=part, dst_ref=red.at[me],
-            send_sem=r_send.at[d], recv_sem=r_recv.at[me],
-            device_id=(d // nsp, d % nsp), device_id_type=MESH)
-
-    def r_arrival(d):
-        return pltpu.make_async_remote_copy(
-            src_ref=part, dst_ref=red.at[d],
-            send_sem=r_send.at[d], recv_sem=r_recv.at[d],
-            device_id=(d // nsp, d % nsp), device_id_type=MESH)
-
-    def res_piece(d):
-        return res.at[pl.ds((d // nsp) * tl, tl), :,
-                      pl.ds(pl.multiple_of((d % nsp) * rows, SUB), rows)]
-
-    def o_copy(d):
-        return pltpu.make_async_remote_copy(
-            src_ref=res_piece(d), dst_ref=out_hbm.at[:, pl.ds(me * own, own)],
-            send_sem=o_send.at[d], recv_sem=o_recv.at[me],
-            device_id=(d // nsp, d % nsp), device_id_type=MESH)
-
-    def o_arrival(d):
-        return pltpu.make_async_remote_copy(
-            src_ref=res_piece(d), dst_ref=out_hbm.at[:, pl.ds(d * own, own)],
-            send_sem=o_send.at[d], recv_sem=o_recv.at[d],
-            device_id=(d // nsp, d % nsp), device_id_type=MESH)
+            src_ref=src, dst_ref=dst, send_sem=sems.at[0], recv_sem=sems.at[1],
+            device_id=(dt, ds), device_id_type=MESH)
+
+    def f_copy(dt, ds):
+        return send(fstage.at[:, dt * nsp + ds],
+                    fwin.at[pl.ds(mt * tl, tl), :, strip(ms)], f_sem, dt, ds)
+
+    def k_copy(dt, ds):
+        return send(kstage.at[ds], kwin.at[:, strip(ms)], k_sem, dt, ds)
+
+    def r_copy(dt, ds):
+        return send(part, red.at[me], r_sem, dt, ds)
+
+    def res_piece(dt, ds):
+        return res.at[pl.ds(dt * tl, tl), :, pl.ds(pl.multiple_of(ds * rows, SUB), rows)]
+
+    def o_copy(dt, ds):
+        return send(res_piece(dt, ds), out_hbm.at[:, pl.ds(me * own, own)], o_sem, dt, ds)
+
+    def await_bytes(ref, sem):
+        pltpu.make_async_copy(ref, ref, sem).wait()
 
     def loop(low, high, act):
         def step(j, carry):
@@ -90,15 +58,24 @@
             return carry
         lax.fori_loop(low, high, step, 0)
 
+    def turn(at, by, size):
+        moved = at + by
+        return jnp.where(moved >= size, moved - size, moved)
+
     def peers(act):
-        loop(1, n, lambda j: act((me + j) % n))
+        for js in range(nsp):
+            ds = turn(ms, js, nsp)
+            for jt in range(ntm):
+                if js or jt:
+                    act(turn(mt, jt, ntm), ds)
 
     def side_peers(act):
-        loop(1, nsp, lambda j: act((ms + j) % nsp))
+        for js in range(1, nsp):
+            act(mt, turn(ms, js, nsp))
 
     barrier = pltpu.get_barrier_semaphore()
-    peers(lambda d: pl.semaphore_signal(
-        barrier, inc=1, device_id=(d // nsp, d % nsp), device_id_type=MESH))
+    peers(lambda dt, ds: pl.semaphore_signal(
+        barrier, inc=1, device_id=(dt, ds), device_id_type=MESH))
     loads = [
         pltpu.make_async_copy(f_hbm, fstage.at[:, :, pl.ds(0, own)], own_sem.at[0]),
         pltpu.make_async_copy(k_hbm, kloc, own_sem.at[1]),
@@ -146,17 +123,16 @@
 
     loop(0, nsp, overlap_k)
     loop(0, n, overlap_f)
-    own_k = pltpu.make_async_copy(kstage.at[ms], kwin.at[:, strip(ms)], own_sem.at[0])
+    own_k = pltpu.make_async_copy(kstage.at[ms], kwin.at[:, strip(ms)], k_sem.at[1])
     own_f = pltpu.make_async_copy(
-        fstage.at[:, me], fwin.at[pl.ds(mt * tl, tl), :, strip(ms)], own_sem.at[1])
+        fstage.at[:, me], fwin.at[pl.ds(mt * tl, tl), :, strip(ms)], f_sem.at[1])
     pl.semaphore_wait(barrier, n - 1)
 
-    side_peers(lambda s: k_copy(s).start())
-    peers(lambda d: f_copy(d).start())
+    side_peers(lambda dt, ds: k_copy(dt, ds).start())
+    peers(lambda dt, ds: f_copy(dt, ds).start())
     own_k.start()
     own_f.start()
-    own_k.wait()
-    side_peers(lambda s: k_arrival(s).wait_recv())
+    await_bytes(kwin.at[:, pl.ds(SUB, nx)], k_sem.at[1])
 
     def lefts(xs):
         turned = [pltpu.roll(x, 1, 1) for x in xs]
@@ -200,8 +176,7 @@
     loop(0, blocks, weights_first)
     loop(0, blocks, weights_second)
 
-    own_f.wait()
-    peers(lambda d: f_arrival(d).wait_recv())
+    await_bytes(fwin.at[:, :, pl.ds(SUB, nx)], f_sem.at[1])
 
     def scale_in(i):
         for c in range(width):
@@ -237,7 +212,7 @@
                 if term is not None and c < own:
                     total = total + term
             return total
-        return lax.fori_loop(0, blocks, block, zero)
+        return lax.fori_loop(0, blocks // 2, lambda i, v: block(2 * i + 1, block(2 * i, v)), zero)
 
     def precondition(q):
         def one(c, i, x, g):
@@ -303,8 +278,8 @@
         row = jnp.where(lane1 == j, value, row)
     part[...] = row
     red[me] = row
-    peers(lambda d: r_copy(d).start())
-    peers(lambda d: r_arrival(d).wait_recv())
+    peers(lambda dt, ds: r_copy(dt, ds).start())
+    await_bytes(red.at[pl.ds(0, n - 1)], r_sem.at[1])
     total = lax.fori_loop(0, n, lambda j, acc: acc + red[j], jnp.zeros((1, LANES), jnp.float32))
     n1, n2, n3, n4, n5, n6 = [
         jnp.sum(jnp.where(lane1 == j, total, 0.0), axis=1, keepdims=True) for j in range(6)]
@@ -333,15 +308,14 @@
 
     loop(0, blocks, finish)
     own_out = pltpu.make_async_copy(
-        res_piece(me), out_hbm.at[:, pl.ds(me * own, own)], own_sem.at[2])
+        res_piece(mt, ms), out_hbm.at[:, pl.ds(me * own, own)], o_sem.at[1])
     own_out.start()
-    peers(lambda d: o_copy(d).start())
-    side_peers(lambda s: k_copy(s).wait_send())
-    peers(lambda d: f_copy(d).wait_send())
-    peers(lambda d: r_copy(d).wait_send())
-    own_out.wait()
-    peers(lambda d: o_arrival(d).wait_recv())
-    peers(lambda d: o_copy(d).wait_send())
+    peers(lambda dt, ds: o_copy(dt, ds).start())
+    await_bytes(kstage.at[pl.ds(0, nsp - 1)], k_sem.at[0])
+    await_bytes(fstage.at[:, pl.ds(0, n - 1)], f_sem.at[0])
+    await_bytes(red.at[pl.ds(0, n - 1)], r_sem.at[0])
+    await_bytes(out_hbm, o_sem.at[1])
+    await_bytes(out_hbm.at[:, pl.ds(0, (n - 1) * own)], o_sem.at[0])
 
 
 def solution(mesh):
@@ -360,6 +334,7 @@
         plain = pltpu.VMEM((width, nx, LANES), jnp.float32)
         field = pltpu.VMEM((steps, width, nx + 2 * SUB, LANES), jnp.float32)
         dma = pltpu.SemaphoreType.DMA
+        f, k = (pltpu.with_memory_space_constraint(x, pltpu.HBM) for x in (f, k))
         out = pl.pallas_call(
             functools.partial(kernel, ntm, nsp),
             out_shape=jax.ShapeDtypeStruct((tl, tiles, rows, LANES), jnp.float32),
@@ -374,8 +349,7 @@
                 pltpu.VMEM((steps, own, nx, LANES), jnp.float32),
                 pltpu.VMEM((1, LANES), jnp.float32),
                 pltpu.VMEM((n, 1, LANES), jnp.float32),
-                dma((n,)), dma((n,)), dma((nsp,)), dma((nsp,)),
-                dma((n,)), dma((n,)), dma((n,)), dma((n,)), dma((3,)),
+                dma((2,)), dma((2,)), dma((2,)), dma((2,)), dma((3,)),
             ],
             compiler_params=pltpu.CompilerParams(
                 collective_id=0, has_side_effects=True, vmem_limit_bytes=24 * 1024 * 1024),

time: 62.9 us -> 51.7 us (0.82)
  the two profiles are of different devices: /device:TPU:0 before, /device:TPU:9 now
where the time goes in v2:
time: 51.7 us; the launch traced here: 51.6 us
  Pallas kernels  50.8 us (98%)
  local copies, waits for them, and re-layouts  0.8 us (2%)
    pallas_call x1, Pallas kernels, body(): pl.pallas_call(functools.partial(kernel, ntm, nsp), out_shape=jax.ShapeDt...  50.8 us

profile of v2, /device:TPU:9, one launch (start us, length us, event | category | flops | bytes accessed | tf_op | source)
XLA Modules:
  0.0 51.6 jit_solution(17044817567444252591)
XLA Ops:
  0.0 50.8 %shard_map.28 = f32[1,128,8,128]{3,2,1,0:T(8,128)S(1)} custom-call(f32[1,32,4,8,128]{4,3,2,1,0:T(8,128)} %bitcast.10, f32[32,4,8,128]{3,2,1,0:T(8,128)} %bitcast.11), custom_call_target="tpu_custom_call" | custom-call | tf_op jit(solution)/shard_map/pallas_call | solution.py:338
  50.8 0.8 %copy.4 = f32[1,8,16384]{2,1,0:T(8,128)} copy(f32[1,8,16384]{2,1,0:T(8,128)S(1)} %bitcast.9) | data formatting | bytes 1048576

commit v3 on v2

--- a/solution.py
+++ b/solution.py
@@ -63,7 +63,7 @@
         return jnp.where(moved >= size, moved - size, moved)
 
     def peers(act):
-        for js in range(nsp):
+        for js in sorted(range(nsp), key=lambda j: abs(j - nsp // 2)):
             ds = turn(ms, js, nsp)
             for jt in range(ntm):
                 if js or jt:
@@ -212,7 +212,14 @@
                 if term is not None and c < own:
                     total = total + term
             return total
-        return lax.fori_loop(0, blocks // 2, lambda i, v: block(2 * i + 1, block(2 * i, v)), zero)
+        group = 8 if blocks % 8 == 0 else 1
+
+        def several(i, total):
+            for j in range(group):
+                total = block(group * i + j, total)
+            return total
+
+        return lax.fori_loop(0, blocks // group, several, zero)
 
     def precondition(q):
         def one(c, i, x, g):

time: 51.7 us -> 47.6 us (0.921)
  the two profiles are of different devices: /device:TPU:9 before, /device:TPU:0 now
where the time goes in v3:
time: 47.6 us; the launch traced here: 47.1 us
  Pallas kernels  46.3 us (97%)
  local copies, waits for them, and re-layouts  0.8 us (2%)
    pallas_call x1, Pallas kernels, body(): pl.pallas_call(functools.partial(kernel, ntm, nsp), out_shape=jax.ShapeDt...  46.3 us

profile of v3, /device:TPU:0, one launch (start us, length us, event | category | flops | bytes accessed | tf_op | source)
XLA Modules:
  0.0 47.1 jit_solution(118528674227568364)
XLA Ops:
  0.0 46.3 %shard_map.28 = f32[1,128,8,128]{3,2,1,0:T(8,128)S(1)} custom-call(f32[1,32,4,8,128]{4,3,2,1,0:T(8,128)} %bitcast.10, f32[32,4,8,128]{3,2,1,0:T(8,128)} %bitcast.11), custom_call_target="tpu_custom_call" | custom-call | tf_op jit(solution)/shard_map/pallas_call | solution.py:345
  46.3 0.8 %copy.4 = f32[1,8,16384]{2,1,0:T(8,128)} copy(f32[1,8,16384]{2,1,0:T(8,128)S(1)} %bitcast.9) | data formatting | bytes 1048576
